TPU v7x, 32 devices: a whole 2x2x4 slice. The times are simulated.
32 devices in a mesh: row: 4 (over y, x), col: 8 (over z, core).
Axes of the slice: x: 2, y: 2, z: 4, core: 2. Of those that a mesh axis runs over, the one named last changes fastest.
Arguments:
- pivot: float32 [1024, 1024], replicated, may hold values from -1 to 2
- col_panel: float32 [2048, 1024], P('row', 'col'), may hold values from -0.25 to 0.25
- row_panel: float32 [1024, 2048], P('row', 'col'), may hold values from -6 to 6
- trailing: float32 [2048, 2048], P('row', 'col'), may hold values from -6 to 6
Outputs:
- updated: float32 [2048, 2048], P('row', 'col')
All inputs are finite; a program needn't handle non-finite values.
Results may differ from a plain program's by a relative error of at most 0.000061.
Values sent between devices are 32-bit elements; how exact they have to be, the bound alone decides.
No kernel may reach another device: no remote copies, remote signals or barrier semaphores. Data moves between devices by JAX's collectives and lax.ppermute only.
A program may use at most 64 MiB of HBM per device.

v0:
```python
import jax
import jax.numpy as jnp
from jax import lax
from jax.sharding import PartitionSpec as P

B = 512


def product(left, right):
    return jnp.dot(left, right, precision=lax.Precision.HIGHEST, preferred_element_type=jnp.float32)


def newton_inverse(matrix):
    identity = jnp.eye(matrix.shape[0], dtype=jnp.float32)
    initial = 2.0 * identity - matrix
    return product(initial, 2.0 * identity - product(matrix, initial))


def local(pivot, col_panel, row_panel, trailing):
    gathered_cols = lax.all_gather(col_panel, "col", axis=1, tiled=True)
    gathered_rows = lax.all_gather(row_panel, "row", axis=0, tiled=True)
    top_left = pivot[:B, :B]
    top_right = pivot[:B, B:]
    low_left = pivot[B:, :B]
    low_right = pivot[B:, B:]
    inverse_one = newton_inverse(top_left)
    multiplier = product(low_left, inverse_one)
    schur = low_right - product(multiplier, top_right)
    inverse_two = newton_inverse(schur)
    factor_one = product(gathered_cols[:, :B], inverse_one)
    factor_two = product(gathered_cols[:, B:] - product(factor_one, top_right), inverse_two)
    first_rows = gathered_rows[:B]
    rows_two = gathered_rows[B:] - product(multiplier, first_rows)
    return trailing - product(factor_one, first_rows) - product(factor_two, rows_two)


def solution(mesh):
    return jax.shard_map(
        local,
        mesh=mesh,
        in_specs=(P(), P("row", "col"), P("row", "col"), P("row", "col")),
        out_specs=P("row", "col"),
        check_vma=False,
    )
```

profile of v0, /device:TPU:9, one launch (start us, length us, event | category | flops | bytes accessed | tf_op | source)
XLA Modules:
  0.0 91.9 jit_solution(5261622955538227202)
XLA Ops:
  6.5 0.0 all-gather.5.cloned.1.call-start
  6.5 0.7 all-gather.5.cloned.1.call-update
  7.3 0.0 all-gather.3.cloned.1.call-start
  7.3 0.7 all-gather.3.cloned.1.call-update
  8.0 0.0 copy-start
  8.0 3.7 %select_subtract_fusion.2 = f32[512,512]{1,0:T(8,128)S(1)} fusion(f32[1024,1024]{1,0:T(8,128)} %param.4), kind=kOutput, calls=%fused_computation.2 | convolution fusion | flops 1612185600 | bytes 3145728 | tf_op jit(solution)/shard_map/dot_general | solution.py:10
  11.7 3.1 %fusion = f32[512,512]{1,0:T(8,128)S(1)} fusion(f32[512,512]{1,0:T(8,128)S(1)} %select_subtract_fusion.2, f32[1024,1024]{1,0:T(8,128)} %param.4), kind=kOutput, calls=%fused_computation.7 | convolution fusion | flops 1611399168 | bytes 3145728 | tf_op jit(solution)/shard_map/dot_general | solution.py:10
  14.9 0.0 copy-done
  14.9 3.5 %fusion.4 = f32[512,512]{1,0:T(8,128)S(1)} fusion(f32[512,512]{1,0:T(8,128)S(1)} %fusion, f32[1024,1024]{1,0:T(8,128)S(1)} %copy-done), kind=kOutput, calls=%fused_computation.14 | convolution fusion | flops 1610612736 | bytes 3145728 | tf_op jit(solution)/shard_map/dot_general | solution.py:10
  18.3 1.8 %convolution_subtract_fusion = f32[512,512]{1,0:T(8,128)S(1)} fusion(f32[512,512]{1,0:T(8,128)S(1)} %fusion.4, f32[1024,1024]{1,0:T(8,128)S(1)} %copy-done), kind=kOutput, calls=%fused_computation.4 | convolution fusion | flops 1610874880 | bytes 4194304 | tf_op jit(solution)/shard_map/dot_general | solution.py:10
  20.2 1.9 %select_subtract_fusion = f32[512,512]{1,0:T(8,128)S(1)} fusion(f32[512,512]{1,0:T(8,128)S(1)} %convolution_subtract_fusion), kind=kOutput, calls=%fused_computation | convolution fusion | flops 1612185600 | bytes 2097152 | tf_op jit(solution)/shard_map/dot_general | solution.py:10
  22.1 2.1 %fusion.1 = f32[512,512]{1,0:T(8,128)S(1)} fusion(f32[512,512]{1,0:T(8,128)S(1)} %select_subtract_fusion, f32[512,512]{1,0:T(8,128)S(1)} %convolution_subtract_fusion), kind=kOutput, calls=%fused_computation.8 | convolution fusion | flops 1611399168 | bytes 3145728 | tf_op jit(solution)/shard_map/dot_general | solution.py:10
  24.2 12.5 %all-gather.5.cloned.1.call-done = f32[1024,256]{1,0:T(8,128)} async-done(((f32[256,256]{1,0:T(8,128)}), f32[1024,256]{1,0:T(8,128)}) %all-gather.5.cloned.1.call-update) | async-done | bytes 1048592 | tf_op jit(solution)/shard_map/all_gather | solution.py:21
  36.7 3.8 %convolution_subtract_fusion.3 = f32[512,256]{1,0:T(8,128)} fusion(f32[512,512]{1,0:T(8,128)S(1)} %fusion.4, f32[1024,256]{1,0:T(8,128)} %all-gather.5.cloned.1.call-done), kind=kOutput, calls=%fused_computation.10 | convolution fusion | flops 805437440 | bytes 2621440 | tf_op jit(solution)/shard_map/dot_general | solution.py:10
  40.5 30.8 %all-gather.3.cloned.1.call-done = f32[512,1024]{1,0:T(8,128)} async-done(((f32[512,128]{1,0:T(8,128)}), f32[512,1024]{1,0:T(8,128)}) %all-gather.3.cloned.1.call-update) | async-done | bytes 2097168 | tf_op jit(solution)/shard_map/all_gather | solution.py:20
  71.3 4.7 %fusion.2 = f32[512,512]{1,0:T(8,128)S(1)} fusion(f32[512,512]{1,0:T(8,128)S(1)} %fusion, f32[512,1024]{1,0:T(8,128)} %all-gather.3.cloned.1.call-done), kind=kOutput, calls=%fused_computation.12 | convolution fusion | flops 1610612736 | bytes 3145728 | tf_op jit(solution)/shard_map/dot_general | solution.py:10
  76.0 0.0 copy-start.2
  76.0 0.0 copy-start.3
  76.0 0.0 copy-start.1
  76.0 3.5 %convolution_subtract_fusion.1 = f32[512,512]{1,0:T(8,128)S(1)} fusion(f32[512,512]{1,0:T(8,128)S(1)} %fusion.2, f32[512,1024]{1,0:T(8,128)} %all-gather.3.cloned.1.call-done, f32[1024,1024]{1,0:T(8,128)} %param.4), kind=kOutput, calls=%fused_computation.5 | convolution fusion | flops 1610874880 | bytes 4194304 | tf_op jit(solution)/shard_map/dot_general | solution.py:10
  79.5 1.8 %fusion.28 = f32[512,512]{1,0:T(8,128)S(1)} fusion(f32[512,512]{1,0:T(8,128)S(1)} %convolution_subtract_fusion.1, f32[512,512]{1,0:T(8,128)S(1)} %fusion.1), kind=kOutput, calls=%fused_computation.39 | convolution fusion | flops 1610612736 | bytes 3145728 | tf_op jit(solution)/shard_map/dot_general | solution.py:10
  81.4 0.0 copy-done.2
  81.4 0.0 copy-done.3
  81.4 1.8 %convolution_subtract_fusion.4 = f32[512,256]{1,0:T(8,128)S(1)} fusion(f32[512,256]{1,0:T(8,128)S(1)} %copy-done.3, f32[512,512]{1,0:T(8,128)S(1)} %fusion.2, f32[1024,256]{1,0:T(8,128)S(1)} %copy-done.2), kind=kOutput, calls=%fused_computation.11 | convolution fusion | flops 805437440 | bytes 2621440 | tf_op jit(solution)/shard_map/dot_general | solution.py:10
  83.2 0.0 copy-done.1
  83.2 1.8 %convolution_subtract_fusion.2 = f32[512,256]{1,0:T(8,128)} fusion(f32[512,256]{1,0:T(8,128)S(1)} %convolution_subtract_fusion.4, f32[512,512]{1,0:T(8,128)S(1)} %fusion.28, f32[512,256]{1,0:T(8,128)S(1)} %copy-done.1), kind=kOutput, calls=%fused_computation.9 | convolution fusion | flops 805437440 | bytes 2621440 | tf_op jit(solution)/shard_map/dot_general | solution.py:10
Async XLA Ops:
  6.5 30.2 %all-gather.5.cloned.1.call-start = ((), (), s32[]{:S(2)}) async-start(), calls=%async_computation.1 | async-start | bytes 1310720 | tf_op jit(solution)/shard_map/all_gather | solution.py:21
  7.3 64.0 %all-gather.3.cloned.1.call-start = ((), (), s32[]{:S(2)}) async-start(), calls=%async_computation | async-start | bytes 2359296 | tf_op jit(solution)/shard_map/all_gather | solution.py:20
  8.0 6.9 %copy-start = (f32[1024,1024]{1,0:T(8,128)S(1)}, f32[1024,1024]{1,0:T(8,128)}, u32[]{:S(2)}) copy-start(f32[1024,1024]{1,0:T(8,128)} %param.4) | copy-start | bytes 12582916
  76.0 5.4 %copy-start.2 = (f32[1024,256]{1,0:T(8,128)S(1)}, f32[1024,256]{1,0:T(8,128)}, u32[]{:S(2)}) copy-start(f32[1024,256]{1,0:T(8,128)} %all-gather.5.cloned.1.call-done) | copy-start | bytes 3145732
  76.0 5.4 %copy-start.3 = (f32[512,256]{1,0:T(8,128)S(1)}, f32[512,256]{1,0:T(8,128)}, u32[]{:S(2)}) copy-start(f32[512,256]{1,0:T(8,128)} %param.7) | copy-start | bytes 1572868
  76.0 7.3 %copy-start.1 = (f32[512,256]{1,0:T(8,128)S(1)}, f32[512,256]{1,0:T(8,128)}, u32[]{:S(2)}) copy-start(f32[512,256]{1,0:T(8,128)} %convolution_subtract_fusion.3) | copy-start | bytes 1572868
Sparse Core Ops, SparseCore 0:
  9.2 27.4 all-gather.4
  38.3 32.9 all-gather.2
where the time goes:
time: 92.1 us; the launch traced here: 91.9 us
  waiting for transfers between devices  44.7 us (49%)
  matrix products  33.6 us (36%)
  between operations  13.5 us (15%)
    dot_general x12, matrix products, product(): jnp.dot(left, right, precision=lax.Precision.HIGHEST, preferred_element_t...  33.6 us
    all_gather x1, waiting for transfers between devices, local(): gathered_cols = lax.all_gather(col_panel, 'col', axis=1, tiled=True)  30.8 us
    all_gather x1, waiting for transfers between devices, local(): gathered_rows = lax.all_gather(row_panel, 'row', axis=0, tiled=True)  12.5 us
  transfers between devices with their start and end apart: 2, of which 2 were waited for; matrix products, arithmetic and copies ran while one was open for 22% of the time, Pallas kernels for 0%

commit v1 on v0

--- a/solution.py
+++ b/solution.py
@@ -18,7 +18,12 @@
 
 def local(pivot, col_panel, row_panel, trailing):
     gathered_cols = lax.all_gather(col_panel, "col", axis=1, tiled=True)
-    gathered_rows = lax.all_gather(row_panel, "row", axis=0, tiled=True)
+    ring = [row_panel]
+    for hop in range(3):
+        ring.append(lax.ppermute(ring[-1], "row", [(dev, (dev + 1) % 4) for dev in range(4)]))
+    gathered_rows = jnp.roll(
+        jnp.concatenate(ring[::-1], axis=0), (lax.axis_index("row") + 1) * ring[0].shape[0], axis=0
+    )
     top_left = pivot[:B, :B]
     top_right = pivot[:B, B:]
     low_left = pivot[B:, :B]

time: 92.1 us -> 63.3 us (0.69)
  waiting for transfers between devices: 44.7 us -> 13.9 us
  starting transfers between devices: 0.04 us -> 2.94 us
  matrix products: 33.6 us -> 31.1 us
  local copies, waits for them, and re-layouts: 0.02 us -> 1.51 us
    all_gather x1, waiting for transfers between devices: 30.8 us -> 3.79 us  [local(): gathered_cols = lax.all_gather(col_panel, 'col', axis=1, tiled=True)]
    all_gather x1 -> x0, waiting for transfers between devices: 12.5 us -> none  [local(): gathered_rows = lax.all_gather(row_panel, 'row', axis=0, tiled=True)]
    ppermute x0 -> x3, waiting for transfers between devices: none -> 9.45 us  [local(): lax.ppermute(ring[-1], 'row', [(dev, (dev + 1) % 4) for dev in range(4)])]
    ppermute x0 -> x3, starting transfers between devices: none -> 2.94 us  [local(): lax.ppermute(ring[-1], 'row', [(dev, (dev + 1) % 4) for dev in range(4)])]
    dot_general x12, matrix products: 33.6 us -> 31.1 us  [product(): jnp.dot(left, right, precision=lax.Precision.HIGHEST, preferred_element_t...]
    unnamed x8 -> x19, local copies, waits for them, and re-layouts: 0.02 us -> 1.49 us
  transfers between devices with their start and end apart: 2 -> 4, of which waited for: 2 -> 3; matrix products, arithmetic and copies ran while one was open for 22% -> 28% of each run, Pallas kernels for 0% -> 0%
where the time goes in v1:
time: 63.3 us; the launch traced here: 63.1 us
  matrix products  31.1 us (49%)
  waiting for transfers between devices  13.9 us (22%)
  between operations  13.6 us (21%)
  starting transfers between devices  2.94 us (5%)
  local copies, waits for them, and re-layouts  1.51 us (2%)
    dot_general x12, matrix products, product(): jnp.dot(left, right, precision=lax.Precision.HIGHEST, preferred_element_t...  31.1 us
    ppermute x3, waiting for transfers between devices, local(): lax.ppermute(ring[-1], 'row', [(dev, (dev + 1) % 4) for dev in range(4)])  9.45 us
    all_gather x1, waiting for transfers between devices, local(): gathered_cols = lax.all_gather(col_panel, 'col', axis=1, tiled=True)  3.79 us
    ppermute x3, starting transfers between devices, local(): lax.ppermute(ring[-1], 'row', [(dev, (dev + 1) % 4) for dev in range(4)])  2.94 us
    unnamed x19, local copies, waits for them, and re-layouts  1.49 us
  transfers between devices with their start and end apart: 4, of which 3 were waited for; matrix products, arithmetic and copies ran while one was open for 28% of the time, Pallas kernels for 0%

profile of v1, /device:TPU:9, one launch (start us, length us, event | category | flops | bytes accessed | tf_op | source)
XLA Modules:
  0.0 63.1 jit_solution(11164768355471604542)
XLA Ops:
  6.5 0.0 all-gather.2.cloned.1.call-start
  6.5 0.7 %all-gather.2.cloned.1.call-update = ((f32[512,128]{1,0:T(8,128)}), f32[512,1024]{1,0:T(8,128)}) async-update(((), (), s32[]{:S(2)}) %all-gather.2.cloned.1.call-start, f32[512,128]{1,0:T(8,128)} %param.5) | async-update | bytes 2621464
  7.3 1.3 %collective-permute-start = (f32[256,256]{1,0:T(8,128)}, f32[256,256]{1,0:T(8,128)S(1)}, u32[]{:S(2)}, u32[]{:S(2)}) collective-permute-start(f32[256,256]{1,0:T(8,128)} %param.6), channel_id=1, source_target_pairs={{0,8},{8,16},{16,24},{24,0},{1,9},{9,17},{17,25},{25,1},{2,10},{10... | collective-permute-start | bytes 786440 | tf_op jit(solution)/shard_map/ppermute | solution.py:23
  8.5 0.0 copy-start
  8.5 3.7 %select_subtract_fusion.2 = f32[512,512]{1,0:T(8,128)S(1)} fusion(f32[1024,1024]{1,0:T(8,128)} %param.4), kind=kOutput, calls=%fused_computation.2 | convolution fusion | flops 1612185600 | bytes 3145728 | tf_op jit(solution)/shard_map/dot_general | solution.py:10
  12.2 3.1 %fusion = f32[512,512]{1,0:T(8,128)S(1)} fusion(f32[512,512]{1,0:T(8,128)S(1)} %select_subtract_fusion.2, f32[1024,1024]{1,0:T(8,128)} %param.4), kind=kOutput, calls=%fused_computation.7 | convolution fusion | flops 1611399168 | bytes 3145728 | tf_op jit(solution)/shard_map/dot_general | solution.py:10
  15.4 0.0 copy-done
  15.4 3.5 %fusion.5 = f32[512,512]{1,0:T(8,128)S(1)} fusion(f32[512,512]{1,0:T(8,128)S(1)} %fusion, f32[1024,1024]{1,0:T(8,128)S(1)} %copy-done), kind=kOutput, calls=%fused_computation.13 | convolution fusion | flops 1610612736 | bytes 3145728 | tf_op jit(solution)/shard_map/dot_general | solution.py:10
  18.9 1.8 %convolution_subtract_fusion = f32[512,512]{1,0:T(8,128)S(1)} fusion(f32[512,512]{1,0:T(8,128)S(1)} %fusion.5, f32[1024,1024]{1,0:T(8,128)S(1)} %copy-done), kind=kOutput, calls=%fused_computation.4 | convolution fusion | flops 1610874880 | bytes 4194304 | tf_op jit(solution)/shard_map/dot_general | solution.py:10
  20.7 0.0 collective-permute-done
  20.7 1.3 %collective-permute-start.1 = (f32[256,256]{1,0:T(8,128)S(1)}, f32[256,256]{1,0:T(8,128)S(1)}, u32[]{:S(2)}, u32[]{:S(2)}) collective-permute-start(f32[256,256]{1,0:T(8,128)S(1)} %collective-permute-done), channel_id=1, source_target_pairs={{0,8},{8,16},{16,24},{24,0},{1,9},{9,17},{17,25},{25,1},{2,10},{10... | collective-permute-start | bytes 786440 | tf_op jit(solution)/shard_map/ppermute | solution.py:23
  22.0 1.9 %select_subtract_fusion = f32[512,512]{1,0:T(8,128)S(1)} fusion(f32[512,512]{1,0:T(8,128)S(1)} %convolution_subtract_fusion), kind=kOutput, calls=%fused_computation | convolution fusion | flops 1612185600 | bytes 2097152 | tf_op jit(solution)/shard_map/dot_general | solution.py:10
  23.9 0.0 copy-start.4
  23.9 4.7 %collective-permute-done.1 = f32[256,256]{1,0:T(8,128)S(1)} collective-permute-done((f32[256,256]{1,0:T(8,128)S(1)}, f32[256,256]{1,0:T(8,128)S(1)}, u32[]{:S(2)}, u32[]{:S(2)}) %collective-permute-start.1) | collective-permute-done | bytes 262176 | tf_op jit(solution)/shard_map/ppermute | solution.py:23
  28.6 0.4 collective-permute-start.2
  29.0 1.9 %fusion.1 = f32[512,512]{1,0:T(8,128)S(1)} fusion(f32[512,512]{1,0:T(8,128)S(1)} %select_subtract_fusion, f32[512,512]{1,0:T(8,128)S(1)} %convolution_subtract_fusion), kind=kOutput, calls=%fused_computation.8 | convolution fusion | flops 1611399168 | bytes 3145728 | tf_op jit(solution)/shard_map/dot_general | solution.py:10
  30.9 4.8 %collective-permute-done.2 = f32[256,256]{1,0:T(8,128)S(1)} collective-permute-done((f32[256,256]{1,0:T(8,128)S(1)}, f32[256,256]{1,0:T(8,128)S(1)}, u32[]{:S(2)}, u32[]{:S(2)}) %collective-permute-start.2) | collective-permute-done | bytes 262176 | tf_op jit(solution)/shard_map/ppermute | solution.py:23
  35.7 0.0 copy-done.4
  35.9 0.0 copy-start.2
  35.9 1.3 %copy-done.2 = f32[2048,256]{1,0:T(8,128)} copy-done((f32[2048,256]{1,0:T(8,128)}, f32[2048,256]{1,0:T(8,128)S(1)}, u32[]{:S(2)}) %copy-start.2) | copy-done | bytes 2097176
  37.2 1.8 %fusion.20 = f32[512,256]{1,0:T(8,128)S(1)} fusion(f32[512,512]{1,0:T(8,128)S(1)} %fusion.5, f32[2048,256]{1,0:T(8,128)S(1)} %constant_dynamic-update-slice_fusion, s32[]{:T(128)S(6)} %select_n.14), kind=kOutput, calls=%fused_computation.30 | convolution fusion | flops 805306368 | bytes 2097156 | tf_op jit(solution)/shard_map/dot_general | solution.py:10
  39.0 3.8 %all-gather.2.cloned.1.call-done = f32[512,1024]{1,0:T(8,128)} async-done(((f32[512,128]{1,0:T(8,128)}), f32[512,1024]{1,0:T(8,128)}) %all-gather.2.cloned.1.call-update) | async-done | bytes 2097168 | tf_op jit(solution)/shard_map/all_gather | solution.py:20
  42.8 0.0 copy-start.1
  42.8 4.8 %fusion.3 = f32[512,512]{1,0:T(8,128)S(1)} fusion(f32[512,512]{1,0:T(8,128)S(1)} %fusion, f32[512,1024]{1,0:T(8,128)} %all-gather.2.cloned.1.call-done), kind=kOutput, calls=%fused_computation.11 | convolution fusion | flops 1610612736 | bytes 3145728 | tf_op jit(solution)/shard_map/dot_general | solution.py:10
  47.6 0.0 copy-done.1
  47.7 3.1 %convolution_subtract_fusion.1 = f32[512,512]{1,0:T(8,128)S(1)} fusion(f32[512,512]{1,0:T(8,128)S(1)} %fusion.3, f32[512,1024]{1,0:T(8,128)S(1)} %copy-done.1, f32[1024,1024]{1,0:T(8,128)} %param.4), kind=kOutput, calls=%fused_computation.5 | convolution fusion | flops 1610874880 | bytes 4194304 | tf_op jit(solution)/shard_map/dot_general | solution.py:10
  50.7 0.0 copy-start.3
  50.7 1.8 %fusion.34 = f32[512,512]{1,0:T(8,128)S(1)} fusion(f32[512,512]{1,0:T(8,128)S(1)} %convolution_subtract_fusion.1, f32[512,512]{1,0:T(8,128)S(1)} %fusion.1), kind=kOutput, calls=%fused_computation.52 | convolution fusion | flops 1610612736 | bytes 3145728 | tf_op jit(solution)/shard_map/dot_general | solution.py:10
  52.6 0.0 copy-done.3
  52.6 0.0 copy-start.5
  52.6 1.0 %fusion.11 = f32[512,256]{1,0:T(8,128)S(1)} fusion(f32[512,512]{1,0:T(8,128)S(1)} %fusion.34, f32[512,256]{1,0:T(8,128)S(1)} %fusion.20, f32[2048,256]{1,0:T(8,128)S(1)} %copy-done.3, s32[]{:T(128)S(6)} %add.16), kind=kOutput, calls=%fused_computation.21 | convolution fusion | flops 805437440 | bytes 2621444 | tf_op jit(solution)/shard_map/dot_general | solution.py:10
  53.6 0.0 copy-done.5
  53.7 2.6 %fusion.2 = f32[512,256]{1,0:T(8,128)} fusion(f32[512,256]{1,0:T(8,128)S(1)} %fusion.11, f32[512,256]{1,0:T(8,128)S(1)} %copy-done.5, f32[512,512]{1,0:T(8,128)S(1)} %fusion.3, f32[2048,256]{1,0:T(8,128)S(1)} %copy-done.3, s32[]{:T(128)S(6)} %select_n.14), kind=kOutput, calls=%fused_computation.10 | convolution fusion | flops 805568512 | bytes 3145732 | tf_op jit(solution)/shard_map/dot_general | solution.py:10
  (8 shorter events, 0.2 us)
Async XLA Ops:
  6.5 36.3 %all-gather.2.cloned.1.call-start = ((), (), s32[]{:S(2)}) async-start(), calls=%async_computation | async-start | bytes 2359296 | tf_op jit(solution)/shard_map/all_gather | solution.py:20
  7.3 13.5 %collective-permute-start = (f32[256,256]{1,0:T(8,128)}, f32[256,256]{1,0:T(8,128)S(1)}, u32[]{:S(2)}, u32[]{:S(2)}) collective-permute-start(f32[256,256]{1,0:T(8,128)} %param.6), channel_id=1, source_target_pairs={{0,8},{8,16},{16,24},{24,0},{1,9},{9,17},{17,25},{25,1},{2,10},{10... | collective-permute-start | bytes 786440 | tf_op jit(solution)/shard_map/ppermute | solution.py:23
  8.5 6.8 %copy-start = (f32[1024,1024]{1,0:T(8,128)S(1)}, f32[1024,1024]{1,0:T(8,128)}, u32[]{:S(2)}) copy-start(f32[1024,1024]{1,0:T(8,128)} %param.4) | copy-start | bytes 12582916
  20.7 7.9 %collective-permute-start.1 = (f32[256,256]{1,0:T(8,128)S(1)}, f32[256,256]{1,0:T(8,128)S(1)}, u32[]{:S(2)}, u32[]{:S(2)}) collective-permute-start(f32[256,256]{1,0:T(8,128)S(1)} %collective-permute-done), channel_id=1, source_target_pairs={{0,8},{8,16},{16,24},{24,0},{1,9},{9,17},{17,25},{25,1},{2,10},{10... | collective-permute-start | bytes 786440 | tf_op jit(solution)/shard_map/ppermute | solution.py:23
  23.9 11.8 %copy-start.4 = (f32[256,256]{1,0:T(8,128)S(1)}, f32[256,256]{1,0:T(8,128)}, u32[]{:S(2)}) copy-start(f32[256,256]{1,0:T(8,128)} %param.6) | copy-start | bytes 786436
  28.6 7.1 %collective-permute-start.2 = (f32[256,256]{1,0:T(8,128)S(1)}, f32[256,256]{1,0:T(8,128)S(1)}, u32[]{:S(2)}, u32[]{:S(2)}) collective-permute-start(f32[256,256]{1,0:T(8,128)S(1)} %collective-permute-done.1), channel_id=1, source_target_pairs={{0,8},{8,16},{16,24},{24,0},{1,9},{9,17},{17,25},{25,1},{2,10},{10... | collective-permute-start | bytes 786440 | tf_op jit(solution)/shard_map/ppermute | solution.py:23
  35.9 1.3 %copy-start.2 = (f32[2048,256]{1,0:T(8,128)}, f32[2048,256]{1,0:T(8,128)S(1)}, u32[]{:S(2)}) copy-start(f32[2048,256]{1,0:T(8,128)S(1)} %constant_dynamic-update-slice_fusion) | copy-start | bytes 6291460
  42.8 4.9 %copy-start.1 = (f32[512,1024]{1,0:T(8,128)S(1)}, f32[512,1024]{1,0:T(8,128)}, u32[]{:S(2)}) copy-start(f32[512,1024]{1,0:T(8,128)} %all-gather.2.cloned.1.call-done) | copy-start | bytes 6291460
  50.7 1.9 %copy-start.3 = (f32[2048,256]{1,0:T(8,128)S(1)}, f32[2048,256]{1,0:T(8,128)}, u32[]{:S(2)}) copy-start(f32[2048,256]{1,0:T(8,128)} %copy-done.2) | copy-start | bytes 6291460
  52.6 1.0 %copy-start.5 = (f32[512,256]{1,0:T(8,128)S(1)}, f32[512,256]{1,0:T(8,128)}, u32[]{:S(2)}) copy-start(f32[512,256]{1,0:T(8,128)} %param.7) | copy-start | bytes 1572868
Sparse Core Ops, SparseCore 0:
  8.9 33.8 all-gather.1
